TPU v7x, 32 devices: a whole 2x2x4 slice. The times are simulated.
32 devices in a mesh: dp: 4 (over x, core), row: 4 (over z), col: 2 (over y).
Axes of the slice: x: 2, y: 2, z: 4, core: 2. Of those that a mesh axis runs over, the one named last changes fastest.
Arguments:
- block_input: bfloat16 [7168, 2048], P(('dp', 'col'), 'row'), may hold values from -6 to 6
- segment_ids: int32 [7168], P(('dp', 'row')), may hold values from 0 to 111, never falling along the last dimension, each value on 1 to 448 neighbouring positions
- attn_gain: float32 [2048], P('row'), may hold values from 0.25 to 1.75
- mix_weight: bfloat16 [2048, 12288], P('row', 'col'), may hold values from -0.125 to 0.125
- decay_weight: bfloat16 [2048, 32], P('row', 'col'), may hold values from -0.125 to 0.125
- conv_weight: float32 [4, 8192], P(None, 'col'), may hold values from -2.5 to 2.5
- decay_log: float32 [16], P('col'), may hold values from -6.5 to -2.5
- decay_bias: float32 [16], P('col'), may hold values from -1.5 to 1
- out_gain: float32 [256], replicated, may hold values from 0.25 to 1.75
- out_weight: bfloat16 [4096, 2048], P('col', 'row'), may hold values from -0.1875 to 0.1875
- ffn_gain: float32 [2048], P('row'), may hold values from 0.25 to 1.75
- gate_weight: bfloat16 [2048, 5632], P('row', 'col'), may hold values from -0.125 to 0.125
- up_weight: bfloat16 [2048, 5632], P('row', 'col'), may hold values from -0.125 to 0.125
- down_weight: bfloat16 [5632, 2048], P('col', 'row'), may hold values from -0.15625 to 0.15625
- cotangent: bfloat16 [7168, 2048], P(('dp', 'col'), 'row'), may hold values from -6 to 6
Outputs:
- block_output: bfloat16 [7168, 2048], P(('dp', 'col'), 'row')
- input_grad: bfloat16 [7168, 2048], P(('dp', 'col'), 'row')
- attn_gain_grad: float32 [2048], P('row')
- mix_weight_grad: float32 [2048, 12288], P('row', 'col')
- decay_weight_grad: float32 [2048, 32], P('row', 'col')
- conv_weight_grad: float32 [4, 8192], P(None, 'col')
- decay_log_grad: float32 [16], P('col')
- decay_bias_grad: float32 [16], P('col')
- out_gain_grad: float32 [256], replicated
- out_weight_grad: float32 [4096, 2048], P('col', 'row')
- ffn_gain_grad: float32 [2048], P('row')
- gate_weight_grad: float32 [2048, 5632], P('row', 'col')
- up_weight_grad: float32 [2048, 5632], P('row', 'col')
- down_weight_grad: float32 [5632, 2048], P('col', 'row')
Inputs may be any that keep to these rules, and one draw needn't show every extreme that they name: `segment_ids`: segment numbers never fall along the tokens; each document has 1 to 448 tokens and one has exactly 448.
All inputs are finite; a program needn't handle non-finite values.
Results may differ from a plain program's by a relative error of at most 0.025.
Values may be sent and summed in bfloat16 or wider, within the bound.
A program may use at most 320 MiB of HBM per device.

v0:
```python
import jax
import jax.numpy as jnp
from jax import lax
from jax.sharding import PartitionSpec as P

D = 2048
BLOCK = 64
SEQ = 448


def block_step(state, inputs):
    query, key, value, beta, decay, starts = inputs
    highest = lax.Precision.HIGHEST
    total = jnp.cumsum(decay, axis=-1)
    marks = jnp.cumsum(starts, axis=-1)
    position = jnp.arange(BLOCK)
    lower = position[:, None] >= position[None, :]
    strict = (position[:, None] > position[None, :]).astype(key.dtype)
    same = (marks[..., :, None] == marks[..., None, :]) & lower
    spread = total[..., :, None] - total[..., None, :]
    weight = jnp.where(same, jnp.exp(jnp.where(same, spread, 0.0)), 0.0)
    carried = jnp.where(marks == 0.0, jnp.exp(total), 0.0)
    inner = jnp.einsum("chtk,chsk->chts", key, key, precision=highest)
    system = jnp.eye(BLOCK, dtype=key.dtype) + beta[..., None] * weight * strict * inner
    known = jnp.einsum("chtk,chkv->chtv", key, state, precision=highest)
    target = beta[..., None] * (value - carried[..., None] * known)
    fresh = jax.scipy.linalg.solve_triangular(system, target, lower=True, unit_diagonal=True)
    scores = jnp.einsum("chtk,chsk->chts", query, key, precision=highest) * weight
    result = carried[..., None] * jnp.einsum("chtk,chkv->chtv", query, state, precision=highest)
    result = result + jnp.einsum("chts,chsv->chtv", scores, fresh, precision=highest)
    last_row = weight[..., -1, :]
    new_state = carried[..., -1][..., None, None] * state
    new_state = new_state + jnp.einsum(
        "chsk,chsv->chkv", key * last_row[..., None], fresh, precision=highest
    )
    return (new_state, result)


def mix_core(proj, decay_in, conv_w, decay_log, decay_bias, out_gain, segments):
    count, length, width = proj.shape
    heads = decay_log.shape[0]
    value_dim = out_gain.shape[0]
    per_head = width // heads
    key_dim = (per_head - 2 * value_dim) // 2
    inner_width = 2 * key_dim + value_dim
    split = proj.reshape(count, length, heads, per_head)
    conv_in = split[..., :inner_width].reshape(count, length, heads * inner_width)
    gate_out = split[..., inner_width:]
    taps = conv_w.shape[0]
    summed = jnp.zeros_like(conv_in)
    for lag in range(taps):
        moved = jnp.pad(conv_in, ((0, 0), (lag, 0), (0, 0)))[:, :length]
        moved_seg = jnp.pad(segments, ((0, 0), (lag, 0)), constant_values=-1)[:, :length]
        keep = (moved_seg == segments).astype(proj.dtype)[..., None]
        summed = summed + conv_w[taps - 1 - lag] * moved * keep
    active = jax.nn.silu(summed).reshape(count, length, heads, inner_width)
    query = active[..., :key_dim]
    key = active[..., key_dim : 2 * key_dim]
    value = active[..., 2 * key_dim :]
    query = (
        query
        * lax.rsqrt(jnp.sum(query * query, axis=-1, keepdims=True) + 1e-06)
        * key_dim ** (-0.5)
    )
    key = key * lax.rsqrt(jnp.sum(key * key, axis=-1, keepdims=True) + 1e-06)
    paired = decay_in.reshape(count, length, heads, 2)
    beta = jax.nn.sigmoid(paired[..., 0])
    decay = -jnp.exp(decay_log) * jax.nn.softplus(paired[..., 1] + decay_bias)
    prior = jnp.pad(segments, ((0, 0), (1, 0)), constant_values=-1)[:, :length]
    starts = jnp.broadcast_to(
        (prior != segments).astype(proj.dtype)[..., None], (count, length, heads)
    )
    blocks = length // BLOCK

    def to_blocks(values):
        values = values.reshape((count, blocks, BLOCK) + values.shape[2:])
        values = jnp.moveaxis(values, 1, 0)
        return jnp.moveaxis(values, 3, 2)

    inputs = (
        to_blocks(query),
        to_blocks(key),
        to_blocks(value),
        to_blocks(beta),
        to_blocks(decay),
        to_blocks(starts),
    )
    state = jnp.zeros((count, heads, key_dim, value_dim), proj.dtype)
    state, outputs = lax.scan(jax.checkpoint(block_step), state, inputs)
    outputs = jnp.moveaxis(jnp.moveaxis(outputs, 3, 2), 0, 1).reshape(
        count, length, heads, value_dim
    )
    normed = outputs * lax.rsqrt(jnp.mean(outputs * outputs, axis=-1, keepdims=True) + 1e-05)
    normed = normed * out_gain * jax.nn.silu(gate_out)
    return normed.reshape(count, length, heads * value_dim)


def project(left, right):
    return jnp.dot(left, right, preferred_element_type=jnp.float32)


def project_back(left, right):
    return jnp.einsum("tn,kn->tk", left, right, preferred_element_type=jnp.float32)


def weight_grad(left, right):
    return jnp.einsum("tk,tn->kn", left, right, preferred_element_type=jnp.float32)


def norm_forward(values):
    local_sum = jnp.sum(values * values, axis=1)
    total = lax.psum(local_sum, "row")
    scale = lax.rsqrt(total / D + 1e-05)[:, None]
    return (values * scale, scale)


def norm_backward(grad_normed, normed, scale, gain):
    scaled = grad_normed * gain
    local_sum = jnp.sum(scaled * normed, axis=1)
    total = lax.psum(local_sum, "row")
    grad_input = scale * (scaled - normed * (total / D)[:, None])
    return (grad_input, jnp.sum(grad_normed * normed, axis=0))


def gather_tokens(values):
    return lax.all_gather(values, "col", axis=0, tiled=True)


def gather_grads(values):
    return lax.all_gather(values, "col", axis=0, tiled=True)


def split_rows(first, second):
    return (
        lax.psum_scatter(first, "row", scatter_dimension=0, tiled=True),
        lax.psum_scatter(second, "row", scatter_dimension=0, tiled=True),
    )


def join_rows(values):
    return lax.all_gather(values, "row", axis=0, tiled=True)


def join_grads(first, second):
    return (
        lax.all_gather(first, "row", axis=0, tiled=True),
        lax.all_gather(second, "row", axis=0, tiled=True),
    )


def sum_to_tokens(whole, weight, out_rows):

    def term(start, count):
        return project(whole, weight)

    return lax.psum_scatter(
        term(jnp.int32(0), lax.axis_size("col") * out_rows).astype(jnp.bfloat16),
        "col",
        scatter_dimension=0,
        tiled=True,
    ).astype(jnp.float32)


def grads_to_tokens(wholes, weights, out_rows):

    def term(start, count):
        total = project_back(wholes[0], weights[0])
        return total + project_back(wholes[1], weights[1])

    return lax.psum_scatter(
        term(jnp.int32(0), lax.axis_size("col") * out_rows).astype(jnp.bfloat16),
        "col",
        scatter_dimension=0,
        tiled=True,
    ).astype(jnp.float32)


def grads_to_rows(whole, weight, out_rows):

    def term(start, count):
        return project_back(whole, weight)

    return lax.psum_scatter(
        term(jnp.int32(0), lax.axis_size("row") * out_rows).astype(jnp.bfloat16),
        "row",
        scatter_dimension=0,
        tiled=True,
    ).astype(jnp.float32)


def swiglu_back(grad_hidden, gate, up_values):
    sigmoid_gate = jax.nn.sigmoid(gate)
    grad_gate = grad_hidden * up_values * sigmoid_gate * (1.0 + gate * (1.0 - sigmoid_gate))
    grad_up = grad_hidden * gate * sigmoid_gate
    return (grad_gate.astype(jnp.bfloat16), grad_up.astype(jnp.bfloat16))


def on_device(
    block_input,
    segment_ids,
    attn_gain,
    mix_weight,
    decay_weight,
    conv_weight,
    decay_log,
    decay_bias,
    out_gain,
    out_weight,
    ffn_gain,
    gate_weight,
    up_weight,
    down_weight,
    cotangent,
):
    stored = block_input.astype(jnp.float32)
    local_rows = stored.shape[0]
    normed_one, scale_one = norm_forward(stored)
    attn_input = (normed_one * attn_gain).astype(jnp.bfloat16)
    attn_all = gather_tokens(attn_input)
    proj, decay_in = split_rows(project(attn_all, mix_weight), project(attn_all, decay_weight))
    mixer_rows = proj.shape[0]
    sequences = mixer_rows // SEQ
    segments = segment_ids.reshape(sequences, SEQ)

    def mixer(proj_rows, decay_rows, conv_local, log_local, bias_local, gain_local):
        result = mix_core(
            proj_rows.reshape(sequences, SEQ, -1),
            decay_rows.reshape(sequences, SEQ, -1),
            conv_local,
            log_local,
            bias_local,
            gain_local,
            segments,
        )
        return result.reshape(mixer_rows, -1)

    mixed, mixer_back = jax.vjp(mixer, proj, decay_in, conv_weight, decay_log, decay_bias, out_gain)
    mixed_all = join_rows(mixed.astype(jnp.bfloat16))
    residual = stored + sum_to_tokens(mixed_all, out_weight, local_rows)
    normed_two, scale_two = norm_forward(residual)
    ffn_input = (normed_two * ffn_gain).astype(jnp.bfloat16)
    ffn_all = gather_tokens(ffn_input)
    gate, up_values = (
        lax.psum(project(ffn_all, gate_weight).astype(jnp.bfloat16), "row").astype(jnp.float32),
        lax.psum(project(ffn_all, up_weight).astype(jnp.bfloat16), "row").astype(jnp.float32),
    )
    hidden_all = (jax.nn.silu(gate) * up_values).astype(jnp.bfloat16)
    block_output = (residual + sum_to_tokens(hidden_all, down_weight, local_rows)).astype(
        jnp.bfloat16
    )
    out_grads = gather_grads(cotangent)
    down_grad = weight_grad(hidden_all, out_grads)
    grad_hidden = lax.psum(project_back(out_grads, down_weight).astype(jnp.bfloat16), "row").astype(
        jnp.float32
    )
    grad_gate, grad_up = swiglu_back(grad_hidden, gate, up_values)
    gate_grad = weight_grad(ffn_all, grad_gate)
    up_grad = weight_grad(ffn_all, grad_up)
    grad_ffn_in = grads_to_tokens((grad_gate, grad_up), (gate_weight, up_weight), local_rows)
    grad_from_ffn, ffn_gain_part = norm_backward(grad_ffn_in, normed_two, scale_two, ffn_gain)
    grad_residual = cotangent.astype(jnp.float32) + grad_from_ffn
    branch_grads = gather_grads(grad_residual.astype(jnp.bfloat16))
    out_weight_grad = weight_grad(mixed_all, branch_grads)
    grad_mixed = grads_to_rows(branch_grads, out_weight, mixer_rows)
    grad_proj, grad_decay_in, conv_part, log_part, bias_part, gain_part = mixer_back(grad_mixed)
    proj_grads, decay_grads = join_grads(
        grad_proj.astype(jnp.bfloat16), grad_decay_in.astype(jnp.bfloat16)
    )
    mix_grad = weight_grad(attn_all, proj_grads)
    decay_grad = weight_grad(attn_all, decay_grads)
    grad_attn_in = grads_to_tokens(
        (proj_grads, decay_grads), (mix_weight, decay_weight), local_rows
    )
    grad_from_attn, attn_gain_part = norm_backward(grad_attn_in, normed_one, scale_one, attn_gain)
    input_grad = (grad_residual + grad_from_attn).astype(jnp.bfloat16)
    summed = (
        lax.psum(mix_grad.astype(jnp.bfloat16), "dp").astype(jnp.float32),
        lax.psum(decay_grad.astype(jnp.bfloat16), "dp").astype(jnp.float32),
        lax.psum(out_weight_grad.astype(jnp.bfloat16), "dp").astype(jnp.float32),
        lax.psum(gate_grad.astype(jnp.bfloat16), "dp").astype(jnp.float32),
        lax.psum(up_grad.astype(jnp.bfloat16), "dp").astype(jnp.float32),
        lax.psum(down_grad.astype(jnp.bfloat16), "dp").astype(jnp.float32),
    )
    row_index = lax.axis_index("row")
    col_index = lax.axis_index("col")
    row_pick = (jnp.arange(lax.axis_size("row")) == row_index).astype(jnp.float32)
    col_pick = (jnp.arange(lax.axis_size("col")) == col_index).astype(jnp.float32)
    small = lax.psum(
        (
            row_pick[:, None] * attn_gain_part[None, :],
            row_pick[:, None] * ffn_gain_part[None, :],
            col_pick[:, None, None] * conv_part[None],
            col_pick[:, None] * log_part[None, :],
            col_pick[:, None] * bias_part[None, :],
            gain_part,
        ),
        ("dp", "row", "col"),
    )
    attn_gain_grad = lax.dynamic_index_in_dim(small[0], row_index, 0, keepdims=False)
    ffn_gain_grad = lax.dynamic_index_in_dim(small[1], row_index, 0, keepdims=False)
    conv_grad = lax.dynamic_index_in_dim(small[2], col_index, 0, keepdims=False)
    log_grad = lax.dynamic_index_in_dim(small[3], col_index, 0, keepdims=False)
    bias_grad = lax.dynamic_index_in_dim(small[4], col_index, 0, keepdims=False)
    return (
        block_output,
        input_grad,
        attn_gain_grad,
        summed[0],
        summed[1],
        conv_grad,
        log_grad,
        bias_grad,
        small[5],
        summed[2],
        ffn_gain_grad,
        summed[3],
        summed[4],
        summed[5],
    )


def solution(mesh):
    return jax.shard_map(
        on_device,
        mesh=mesh,
        in_specs=(
            P(("dp", "col"), "row"),
            P(("dp", "row")),
            P("row"),
            P("row", "col"),
            P("row", "col"),
            P(None, "col"),
            P("col"),
            P("col"),
            P(),
            P("col", "row"),
            P("row"),
            P("row", "col"),
            P("row", "col"),
            P("col", "row"),
            P(("dp", "col"), "row"),
        ),
        out_specs=(
            P(("dp", "col"), "row"),
            P(("dp", "col"), "row"),
            P("row"),
            P("row", "col"),
            P("row", "col"),
            P(None, "col"),
            P("col"),
            P("col"),
            P(),
            P("col", "row"),
            P("row"),
            P("row", "col"),
            P("row", "col"),
            P("col", "row"),
        ),
        check_vma=False,
    )
```

profile of v0, /device:TPU:0, one launch (start us, length us, event | category | flops | bytes accessed | tf_op | source)
XLA Modules:
  0.0 4328.8 jit_solution(5476020139172058934)
XLA Ops:
  8.8 13.5 psum.133
  25.4 28.5 all-gather.8.cloned.1.call-done
  56.9 22.5 fusion.207
  84.8 718.7 %reduce-scatter.10.cloned.1.call-done = f32[448,6144]{1,0:T(8,128)} async-done(((f32[1792,6144]{1,0:T(8,128)}), f32[448,6144]{1,0:T(8,128)}) %reduce-scatter.10.cloned.1.call-update) | async-done | bytes 11010064 | tf_op jit(solution)/shard_map/reduce_scatter | solution.py:135
  803.4 13.4 copy.432
  823.8 9.0 reshape.1399
  832.9 17.5 fusion.161
  850.4 7.0 copy.433
  874.3 405.6 %while.44 = (s32[]{:T(128)}, f32[1,8,128,256]{3,2,1,0:T(8,128)}, f32[7,1,8,64,256]{4,2,3,0,1:T(8,128)}, f32[7,1,8,128,256]{4,3,2,1,0:T(8,128)}, f32[7,1,8,64]{3,...) while((s32[]{:T(128)}, f32[1,8,128,256]{3,2,1,0:T(8,128)}, ...), condition=%wide.region_9.11_spmd.clone.clone, body=%wide.region_6.10_spmd.clone.clone.sunk | while | flops 908922432 | bytes 18620180 | solution.py:89
  877.6 40.0 custom-call.26
  933.9 40.0 custom-call.26
  992.0 40.0 custom-call.26
  1050.2 40.0 custom-call.26
  1108.4 40.0 custom-call.26
  1166.6 40.0 custom-call.26
  1224.7 40.0 custom-call.26
  1288.5 134.2 %all-gather.10.cloned.1.call-done = bf16[1792,2048]{1,0:T(8,128)(2,1)} async-done(((bf16[448,2048]{1,0:T(8,128)(2,1)}), bf16[1792,2048]{1,0:T(8,128)(2,1)}) %all-gather.10.cloned.1.call-update) | async-done | bytes 7340048 | tf_op jit(solution)/shard_map/all_gather | solution.py:141
  1422.7 8.9 convolution_convert_fusion.9
  1432.3 26.7 reduce-scatter.12.cloned.1.call-done
  1460.8 11.9 psum.134
  1475.5 15.1 all-gather.14.cloned.1.call-done
  1490.6 10.0 convolution_convert_fusion
  1500.6 22.3 all-gather.12.cloned.1.call-done
  1522.9 10.2 convolution_convert_fusion.1
  1533.1 7.8 convolution_convert_fusion.2
  1540.9 1000.2 %all-reduce.31.cloned.1.call-done = (bf16[1792,2816]{1,0:T(8,128)(2,1)}, bf16[1792,2816]{1,0:T(8,128)(2,1)}, bf16[1792,2816]{1,0:T(8,128)(2,1)}) async-done(((bf16[1792,2816]{1,0:T(8,128)(2,1)}, bf16[1792,2816]{1,0:T(8,128)(2,1)}, bf16[1792,2816]{1,0:T(8,128)(2,1)}), (bf16[1792,2816]{1,0:T(8,128)(2,1)}, bf16[1792,2816]{1,0:T(8,128)(2,1)}, bf16[1792,2816]{1,0:T(8,128)(2,1)})) %all-reduce.31.cloned.1.call-update) | async-done | bytes 30277648 | tf_op jit(solution)/shard_map/psum | solution.py:245
  2541.1 18.6 fusion.155
  2559.7 8.2 fusion.208
  2568.3 8.5 add_convert_fusion.2
  2576.8 27.9 reduce-scatter.16.cloned.1.call-done
  2607.4 11.7 psum.138
  2622.3 27.1 all-gather.16.cloned.1.call-done
  2649.4 9.1 convolution_convert_fusion.4
  2658.7 127.8 %reduce-scatter.18.cloned.1.call-done = bf16[448,2048]{1,0:T(8,128)(2,1)} async-done(((bf16[1792,2048]{1,0:T(8,128)(2,1)}), bf16[448,2048]{1,0:T(8,128)(2,1)}) %reduce-scatter.18.cloned.1.call-update) | async-done | bytes 1835024 | tf_op jit(solution)/shard_map/reduce_scatter | solution.py:183
  2788.4 8.4 multiply_reduce_fusion.8
  2808.8 547.6 %while.43 = (s32[]{:T(128)}, f32[1,8,128,256]{2,3,1,0:T(8,128)}, f32[7,1,8,64,128]{4,2,3,0,1:T(8,128)}, f32[7,1,8,64,128]{4,2,3,0,1:T(8,128)}, f32[7,1,8,64,256]...) while((s32[]{:T(128)}, f32[1,8,128,256]{2,3,1,0:T(8,128)}, ...), condition=%wide.region_35.37_spmd.clone, body=%wide.region_23.36_spmd.clone.sunk | while | flops 2448786944 | bytes 53756548 | solution.py:89
  2819.4 40.7 custom-call.25
  2897.7 40.7 custom-call.25
  2976.0 40.7 custom-call.25
  3054.3 40.7 custom-call.25
  3132.7 40.7 custom-call.25
  3211.0 40.7 custom-call.25
  3289.3 40.7 custom-call.25
  3370.3 9.0 reshape.1411
  3379.3 17.2 multiply_reduce_fusion.7
  3396.6 8.2 multiply_multiply_fusion.2
  3404.8 9.3 fusion.158
  3414.1 10.1 copy.436
  3424.2 7.2 add_convert_fusion
  3439.2 13.7 all-gather
  3456.5 356.3 %all-gather.18.cloned.1.call-done = bf16[1792,6144]{1,0:T(8,128)(2,1)} async-done(((bf16[448,6144]{1,0:T(8,128)(2,1)}), bf16[1792,6144]{1,0:T(8,128)(2,1)}) %all-gather.18.cloned.1.call-update) | async-done | bytes 22020112 | tf_op jit(solution)/shard_map/all_gather | solution.py:146
  3812.9 19.4 add_convert_fusion.1
  3832.3 9.8 convolution_convert_fusion.10
  3842.2 11.6 convolution_convert_fusion.6
  3853.9 10.9 convolution_convert_fusion.5
  3864.8 7.0 convolution_convert_fusion.7
  3877.0 17.9 convolution_convert_fusion.3
  3897.0 11.2 psum.142
  3909.2 30.7 all-reduce.29.cloned.1.call-done
  3941.3 28.6 reduce-scatter.20.cloned.1.call-done
  3972.0 40.0 all-reduce.22
  4012.1 10.6 psum.139
  4028.7 272.0 %all-reduce.33.cloned.1.call-done = (bf16[512,6144]{1,0:T(8,128)(2,1)}, bf16[2048,512]{1,0:T(8,128)(2,1)}, bf16[512,2816]{1,0:T(8,128)(2,1)}, bf16[512,2816]{1,0:T(8,128)(2,1)}, bf16[2816,512]{1,0:T(8,128)(2,1)}) async-done(((bf16[512,6144]{1,0:T(8,128)(2,1)}, bf16[2048,512]{1,0:T(8,128)(2,1)}, bf16[512,2816]{1,0:T(8,128)(2,1)}, bf16[512,2816]{1,0:T(8,128)(2,1)}, bf16[2816,512]{1,0:T(8,128)(2,1)}), ...) | async-done | bytes 17039376 | tf_op jit(solution)/shard_map/psum | solution.py:277
  4300.6 9.4 convert_element_type.246
  (963 shorter events, 510.6 us)
Async XLA Ops:
  7.2 1525.9 %copy-start = (bf16[512,2816]{1,0:T(8,128)(2,1)S(1)}, bf16[512,2816]{1,0:T(8,128)(2,1)}, u32[]{:S(2)}) copy-start(bf16[512,2816]{1,0:T(8,128)(2,1)} %param.32) | copy-start | bytes 8650756
  7.2 46.6 %copy-start.50 = (bf16[512,16]{0,1:T(8,128)(2,1)S(1)}, bf16[512,16]{0,1:T(8,128)(2,1)}, u32[]{:S(2)}) copy-start(bf16[512,16]{0,1:T(8,128)(2,1)} %param.25) | copy-start | bytes 49156
  7.2 46.6 %all-gather.8.cloned.1.call-start = ((), (), s32[]{:S(2)}) async-start(), calls=%async_computation.7 | async-start | bytes 2752512 | tf_op jit(solution)/shard_map/all_gather | solution.py:126
  25.3 56.8 %reduce-scatter.22.cloned.1.call-start = ((), (), s32[]{:S(2)}) async-start(), calls=%async_computation.20 | async-start | bytes 1146880
  56.9 746.6 %reduce-scatter.10.cloned.1.call-start = ((), (), s32[]{:S(2)}) async-start(), calls=%async_computation.8 | async-start | bytes 55050240 | tf_op jit(solution)/shard_map/reduce_scatter | solution.py:135
  79.5 1343.3 %all-gather.10.cloned.1.call-start = ((), (), s32[]{:S(2)}) async-start(), calls=%async_computation.9 | async-start | bytes 9175040 | tf_op jit(solution)/shard_map/all_gather | solution.py:141
  80.3 736.6 %copy-start.71 = (f32[8]{0:T(128)}, f32[8]{0:T(128)S(1)}, u32[]{:S(2)}) copy-start(f32[8]{0:T(128)S(1)} %exponential_negate_fusion) | copy-start | bytes 100
  80.4 752.5 %copy-start.57 = (f32[1,448]{1,0:T(1,128)}, f32[1,448]{1,0:T(1,128)S(1)}, u32[]{:S(2)}) copy-start(f32[1,448]{1,0:T(1,128)S(1)} %get-tuple-element.925) | copy-start | bytes 5380
  80.4 752.5 %copy-start.59 = (f32[1,448]{1,0:T(1,128)}, f32[1,448]{1,0:T(1,128)S(1)}, u32[]{:S(2)}) copy-start(f32[1,448]{1,0:T(1,128)S(1)} %get-tuple-element.926) | copy-start | bytes 5380
  80.4 752.5 %copy-start.61 = (f32[1,448]{1,0:T(1,128)}, f32[1,448]{1,0:T(1,128)S(1)}, u32[]{:S(2)}) copy-start(f32[1,448]{1,0:T(1,128)S(1)} %get-tuple-element.927) | copy-start | bytes 5380
  80.5 752.4 %copy-start.31 = (f32[1,4096]{1,0:T(1,128)}, f32[1,4096]{1,0:T(1,128)S(1)}, u32[]{:S(2)}) copy-start(f32[1,4096]{1,0:T(1,128)S(1)} %get-tuple-element.917) | copy-start | bytes 49156
  80.5 752.4 %copy-start.33 = (f32[1,4096]{1,0:T(1,128)}, f32[1,4096]{1,0:T(1,128)S(1)}, u32[]{:S(2)}) copy-start(f32[1,4096]{1,0:T(1,128)S(1)} %get-tuple-element.918) | copy-start | bytes 49156
  80.5 752.4 %copy-start.35 = (f32[1,4096]{1,0:T(1,128)}, f32[1,4096]{1,0:T(1,128)S(1)}, u32[]{:S(2)}) copy-start(f32[1,4096]{1,0:T(1,128)S(1)} %get-tuple-element.919) | copy-start | bytes 49156
  80.5 752.4 %copy-start.37 = (f32[1,4096]{1,0:T(1,128)}, f32[1,4096]{1,0:T(1,128)S(1)}, u32[]{:S(2)}) copy-start(f32[1,4096]{1,0:T(1,128)S(1)} %get-tuple-element.920) | copy-start | bytes 49156
  83.3 733.6 %copy-start.39 = (f32[1,448,8,1]{1,3,2,0:T(1,128)}, f32[1,448,8,1]{1,3,2,0:T(1,128)S(1)}, u32[]{:S(2)}) copy-start(f32[1,448,8,1]{1,3,2,0:T(1,128)S(1)} %get-tuple-element.921) | copy-start | bytes 43012
  84.0 732.9 %copy-start.29 = (f32[1,7,64,8]{2,1,3,0:T(8,128)}, f32[1,7,64,8]{2,1,3,0:T(8,128)S(1)}, u32[]{:S(2)}) copy-start(f32[1,7,64,8]{2,1,3,0:T(8,128)S(1)} %squeeze.150) | copy-start | bytes 43012
  1288.5 170.5 %reduce-scatter.12.cloned.1.call-start = ((), (), s32[]{:S(2)}) async-start(), calls=%async_computation.10 | async-start | bytes 2752512 | tf_op jit(solution)/shard_map/reduce_scatter | solution.py:156
  1431.6 41.1 copy-start.63
  1431.6 58.9 %all-gather.14.cloned.1.call-start = ((), (), s32[]{:S(2)}) async-start(), calls=%async_computation.13 | async-start | bytes 2752512 | tf_op jit(solution)/shard_map/all_gather | solution.py:130
  1432.2 90.7 %all-gather.12.cloned.1.call-start = ((), (), s32[]{:S(2)}) async-start(), calls=%async_computation.11 | async-start | bytes 2752512 | tf_op jit(solution)/shard_map/all_gather | solution.py:126
  1472.7 1146.3 %copy-start.48 = (f32[896]{0:T(1024)}, f32[896]{0:T(1024)S(1)}, u32[]{:S(2)}) copy-start(f32[896]{0:T(1024)S(1)} %add_rsqrt_fusion.2) | copy-start | bytes 10756
  1475.4 1065.7 %all-reduce.31.cloned.1.call-start = ((), (), s32[]{:S(2)}) async-start(), calls=%async_computation.21 | async-start | bytes 60555264 | tf_op jit(solution)/shard_map/psum | solution.py:245
  1540.9 1063.8 %reduce-scatter.16.cloned.1.call-start = ((), (), s32[]{:S(2)}) async-start(), calls=%async_computation.14 | async-start | bytes 2752512 | tf_op jit(solution)/shard_map/reduce_scatter | solution.py:170
  2568.3 36.5 copy-start.10
  2568.3 36.5 copy-start.13
  2576.8 42.3 copy-start.20
  2576.8 72.7 %all-gather.16.cloned.1.call-start = ((), (), s32[]{:S(2)}) async-start(), calls=%async_computation.15 | async-start | bytes 2752512 | tf_op jit(solution)/shard_map/all_gather | solution.py:130
  2619.0 39.6 copy-start.55
  2621.9 164.6 %reduce-scatter.18.cloned.1.call-start = ((), (), s32[]{:S(2)}) async-start(), calls=%async_computation.16 | async-start | bytes 9175040 | tf_op jit(solution)/shard_map/reduce_scatter | solution.py:183
  2658.6 1154.2 %all-gather.18.cloned.1.call-start = ((), (), s32[]{:S(2)}) async-start(), calls=%async_computation.17 | async-start | bytes 27525120 | tf_op jit(solution)/shard_map/all_gather | solution.py:146
  2814.7 48.9 %copy-start.3 = (f32[1,8,64,128]{3,2,1,0:T(8,128)}, f32[1,8,64,128]{3,2,1,0:T(8,128)S(1)}, u32[]{:S(2)}) copy-start(f32[1,8,64,128]{3,2,1,0:T(8,128)S(1)} %dynamic-slice_bitcast_fusion.18) | copy-start | bytes 786436 | tf_op jit(solution)/shard_map/transpose(jvp())/while
  2817.8 49.1 %copy-start.6 = (f32[8,64,64]{2,1,0:T(8,128)}, f32[8,64,64]{2,1,0:T(8,128)S(1)}, u32[]{:S(2)}) copy-start(f32[8,64,64]{2,1,0:T(8,128)S(1)} %fusion.368) | copy-start | bytes 393220 | tf_op jit(solution)/shard_map/transpose(jvp())/while
  2891.8 50.2 %copy-start.3 = (f32[1,8,64,128]{3,2,1,0:T(8,128)}, f32[1,8,64,128]{3,2,1,0:T(8,128)S(1)}, u32[]{:S(2)}) copy-start(f32[1,8,64,128]{3,2,1,0:T(8,128)S(1)} %dynamic-slice_bitcast_fusion.18) | copy-start | bytes 786436 | tf_op jit(solution)/shard_map/transpose(jvp())/while
  2896.1 49.1 %copy-start.6 = (f32[8,64,64]{2,1,0:T(8,128)}, f32[8,64,64]{2,1,0:T(8,128)S(1)}, u32[]{:S(2)}) copy-start(f32[8,64,64]{2,1,0:T(8,128)S(1)} %fusion.368) | copy-start | bytes 393220 | tf_op jit(solution)/shard_map/transpose(jvp())/while
  2970.1 50.2 %copy-start.3 = (f32[1,8,64,128]{3,2,1,0:T(8,128)}, f32[1,8,64,128]{3,2,1,0:T(8,128)S(1)}, u32[]{:S(2)}) copy-start(f32[1,8,64,128]{3,2,1,0:T(8,128)S(1)} %dynamic-slice_bitcast_fusion.18) | copy-start | bytes 786436 | tf_op jit(solution)/shard_map/transpose(jvp())/while
  2974.4 49.1 %copy-start.6 = (f32[8,64,64]{2,1,0:T(8,128)}, f32[8,64,64]{2,1,0:T(8,128)S(1)}, u32[]{:S(2)}) copy-start(f32[8,64,64]{2,1,0:T(8,128)S(1)} %fusion.368) | copy-start | bytes 393220 | tf_op jit(solution)/shard_map/transpose(jvp())/while
  3048.4 50.2 %copy-start.3 = (f32[1,8,64,128]{3,2,1,0:T(8,128)}, f32[1,8,64,128]{3,2,1,0:T(8,128)S(1)}, u32[]{:S(2)}) copy-start(f32[1,8,64,128]{3,2,1,0:T(8,128)S(1)} %dynamic-slice_bitcast_fusion.18) | copy-start | bytes 786436 | tf_op jit(solution)/shard_map/transpose(jvp())/while
  3052.8 49.1 %copy-start.6 = (f32[8,64,64]{2,1,0:T(8,128)}, f32[8,64,64]{2,1,0:T(8,128)S(1)}, u32[]{:S(2)}) copy-start(f32[8,64,64]{2,1,0:T(8,128)S(1)} %fusion.368) | copy-start | bytes 393220 | tf_op jit(solution)/shard_map/transpose(jvp())/while
  3126.8 50.2 %copy-start.3 = (f32[1,8,64,128]{3,2,1,0:T(8,128)}, f32[1,8,64,128]{3,2,1,0:T(8,128)S(1)}, u32[]{:S(2)}) copy-start(f32[1,8,64,128]{3,2,1,0:T(8,128)S(1)} %dynamic-slice_bitcast_fusion.18) | copy-start | bytes 786436 | tf_op jit(solution)/shard_map/transpose(jvp())/while
  3131.1 49.1 %copy-start.6 = (f32[8,64,64]{2,1,0:T(8,128)}, f32[8,64,64]{2,1,0:T(8,128)S(1)}, u32[]{:S(2)}) copy-start(f32[8,64,64]{2,1,0:T(8,128)S(1)} %fusion.368) | copy-start | bytes 393220 | tf_op jit(solution)/shard_map/transpose(jvp())/while
  3205.1 50.2 %copy-start.3 = (f32[1,8,64,128]{3,2,1,0:T(8,128)}, f32[1,8,64,128]{3,2,1,0:T(8,128)S(1)}, u32[]{:S(2)}) copy-start(f32[1,8,64,128]{3,2,1,0:T(8,128)S(1)} %dynamic-slice_bitcast_fusion.18) | copy-start | bytes 786436 | tf_op jit(solution)/shard_map/transpose(jvp())/while
  3209.4 49.1 %copy-start.6 = (f32[8,64,64]{2,1,0:T(8,128)}, f32[8,64,64]{2,1,0:T(8,128)S(1)}, u32[]{:S(2)}) copy-start(f32[8,64,64]{2,1,0:T(8,128)S(1)} %fusion.368) | copy-start | bytes 393220 | tf_op jit(solution)/shard_map/transpose(jvp())/while
  3283.4 50.1 %copy-start.3 = (f32[1,8,64,128]{3,2,1,0:T(8,128)}, f32[1,8,64,128]{3,2,1,0:T(8,128)S(1)}, u32[]{:S(2)}) copy-start(f32[1,8,64,128]{3,2,1,0:T(8,128)S(1)} %dynamic-slice_bitcast_fusion.18) | copy-start | bytes 786436 | tf_op jit(solution)/shard_map/transpose(jvp())/while
  3287.7 49.1 %copy-start.6 = (f32[8,64,64]{2,1,0:T(8,128)}, f32[8,64,64]{2,1,0:T(8,128)S(1)}, u32[]{:S(2)}) copy-start(f32[8,64,64]{2,1,0:T(8,128)S(1)} %fusion.368) | copy-start | bytes 393220 | tf_op jit(solution)/shard_map/transpose(jvp())/while
  3379.3 17.3 copy-start.34
  3379.3 17.3 copy-start.36
  3379.3 17.3 copy-start.38
  3438.2 501.6 %all-reduce.29.cloned.1.call-start = ((), (), s32[]{:S(2)}) async-start(), calls=%async_computation.19 | async-start | bytes 262144 | tf_op jit(solution)/shard_map/psum | solution.py:288
  3456.5 513.5 %reduce-scatter.20.cloned.1.call-start = ((), (), s32[]{:S(2)}) async-start(), calls=%async_computation.18 | async-start | bytes 2752512 | tf_op jit(solution)/shard_map/reduce_scatter | solution.py:170
  3832.2 192.6 %reduce-scatter.14.cloned.1.call-start = ((), (), s32[]{:S(2)}) async-start(), calls=%async_computation.12 | async-start | bytes 2752512 | tf_op jit(solution)/shard_map/reduce_scatter | solution.py:156
  3842.2 458.5 %all-reduce.33.cloned.1.call-start = ((), (), s32[]{:S(2)}) async-start(), calls=%async_computation.22 | async-start | bytes 34078720 | tf_op jit(solution)/shard_map/psum | solution.py:277
  3842.2 22.5 slice-start
  3842.2 29.6 slice-start.3
  3853.9 17.9 slice-start.4
  3894.9 75.1 %copy-start.11 = (bf16[896,512]{1,0:T(8,128)(2,1)S(1)}, bf16[896,512]{1,0:T(8,128)(2,1)}, u32[]{:S(2)}) copy-start(bf16[896,512]{1,0:T(8,128)(2,1)} %param.21) | copy-start | bytes 2752516
  3894.9 75.1 %copy-start.53 = (f32[896]{0:T(1024)S(1)}, f32[896]{0:T(1024)}, u32[]{:S(2)}) copy-start(f32[896]{0:T(1024)} %copy-done.52) | copy-start | bytes 10756
  3894.9 75.0 %copy-start.65 = (f32[512]{0:T(512)S(1)}, f32[512]{0:T(512)}, u32[]{:S(2)}) copy-start(f32[512]{0:T(512)} %param.23) | copy-start | bytes 6148
  3894.9 77.0 %copy-start.68 = (f32[512]{0:T(512)S(1)}, f32[512]{0:T(512)}, u32[]{:S(2)}) copy-start(f32[512]{0:T(512)} %get-tuple-element.811) | copy-start | bytes 6148
  3895.0 77.1 %copy-start.73 = (f32[256]{0:T(256)S(1)}, f32[256]{0:T(256)}, u32[]{:S(2)}) copy-start(f32[256]{0:T(256)} %get-tuple-element.801) | copy-start | bytes 3076
  3895.0 129.9 %copy-start.14 = (bf16[896,512]{1,0:T(8,128)(2,1)S(1)}, bf16[896,512]{1,0:T(8,128)(2,1)}, u32[]{:S(2)}) copy-start(bf16[896,512]{1,0:T(8,128)(2,1)} %reduce-scatter.12.cloned.1.call-done) | copy-start | bytes 2752516
  3895.0 129.9 %copy-start.21 = (bf16[896,512]{1,0:T(8,128)(2,1)S(1)}, bf16[896,512]{1,0:T(8,128)(2,1)}, u32[]{:S(2)}) copy-start(bf16[896,512]{1,0:T(8,128)(2,1)} %param.35) | copy-start | bytes 2752516
  3895.0 129.9 %copy-start.49 = (f32[896]{0:T(1024)S(1)}, f32[896]{0:T(1024)}, u32[]{:S(2)}) copy-start(f32[896]{0:T(1024)} %copy-done.48) | copy-start | bytes 10756
  3895.0 129.9 %copy-start.56 = (f32[896]{0:T(1024)S(1)}, f32[896]{0:T(1024)}, u32[]{:S(2)}) copy-start(f32[896]{0:T(1024)} %copy-done.55) | copy-start | bytes 10756
  3895.0 129.9 %copy-start.64 = (f32[512]{0:T(512)S(1)}, f32[512]{0:T(512)}, u32[]{:S(2)}) copy-start(f32[512]{0:T(512)} %param.31) | copy-start | bytes 6148
  (80 other events, 416.4 us)
Sparse Core Ops, SparseCore 0:
  25.4 28.3 all-gather.7
  57.0 25.0 reduce-scatter.21
  84.5 718.8 reduce-scatter.9
  1288.6 134.0 all-gather.9
  1431.7 27.1 reduce-scatter.11
  1460.4 30.1 all-gather.13
  1492.7 30.1 all-gather.11
  1541.0 1000.0 all-reduce.30
  2576.9 27.7 reduce-scatter.15
  2622.0 27.3 all-gather.15
  2658.7 127.7 reduce-scatter.17
  3438.3 374.4 all-gather.17
  3819.0 120.8 all-reduce.28
  3941.9 27.9 reduce-scatter.19
  3972.1 29.4 reduce-scatter.13
  4005.7 294.9 all-reduce.32
where the time goes:
time: 4340 us; the launch traced here: 4330 us
  waiting for transfers between devices  2820 us (65%)
  other arithmetic  776 us (18%)
  matrix products  417 us (10%)
  local copies, waits for them, and re-layouts  184 us (4%)
  blocking collectives  112 us (3%)
    psum x1, waiting for transfers between devices, on_device(): lax.psum(project(ffn_all, up_weight).astype(jnp.bfloat16), 'row')  1000 us
    reduce_scatter x1, waiting for transfers between devices, split_rows(): lax.psum_scatter(first, 'row', scatter_dimension=0, tiled=True)  719 us
    another operation x56, other arithmetic, block_step(): jax.scipy.linalg.solve_triangular(system, target, lower=True, unit_diagon...  573 us
    all_gather x1, waiting for transfers between devices, join_grads(): lax.all_gather(first, 'row', axis=0, tiled=True)  356 us
    psum x1, waiting for transfers between devices, on_device(): lax.psum(mix_grad.astype(jnp.bfloat16), 'dp').astype(jnp.float32)  272 us
    all_gather x1, waiting for transfers between devices, join_rows(): return lax.all_gather(values, 'row', axis=0, tiled=True)  134 us
    reduce_scatter x1, waiting for transfers between devices, grads_to_rows(): lax.psum_scatter(term(jnp.int32(0), lax.axis_size('row') * out_rows).asty...  128 us
  transfers between devices with their start and end apart: 16, of which 15 were waited for; matrix products, arithmetic and copies ran while one was open for 3% of the time, Pallas kernels for 0%

commit v1 on v0

--- a/solution.py
+++ b/solution.py
@@ -138,7 +138,9 @@
 
 
 def join_rows(values):
-    return lax.all_gather(values, "row", axis=0, tiled=True)
+    return jnp.concatenate(
+        lax.all_to_all(jnp.stack([values] * lax.axis_size("row")), "row", 0, 0), axis=0
+    )
 
 
 def join_grads(first, second):

time: 4340 us -> 4370 us (level)
  blocking collectives: 112 us -> 278 us
  waiting for transfers between devices: 2820 us -> 2690 us
    all_to_all x0 -> x1, blocking collectives: none -> 166 us  [join_rows(): lax.all_to_all(jnp.stack([values] * lax.axis_size('row')), 'row', 0, 0)]
    all_gather x1 -> x0, waiting for transfers between devices: 134 us -> none  [join_rows(): return lax.all_gather(values, 'row', axis=0, tiled=True)]
  transfers between devices with their start and end apart: 16 -> 15, of which waited for: 15 -> 14; matrix products, arithmetic and copies ran while one was open for 3% -> 3% of each run, Pallas kernels for 0% -> 0%
where the time goes in v1:
time: 4370 us; the launch traced here: 4360 us
  waiting for transfers between devices  2690 us (62%)
  other arithmetic  776 us (18%)
  matrix products  413 us (9%)
  blocking collectives  278 us (6%)
  local copies, waits for them, and re-layouts  187 us (4%)
    psum x1, waiting for transfers between devices, on_device(): lax.psum(project(ffn_all, up_weight).astype(jnp.bfloat16), 'row')  1000 us
    reduce_scatter x1, waiting for transfers between devices, split_rows(): lax.psum_scatter(first, 'row', scatter_dimension=0, tiled=True)  719 us
    another operation x56, other arithmetic, block_step(): jax.scipy.linalg.solve_triangular(system, target, lower=True, unit_diagon...  573 us
    all_gather x1, waiting for transfers between devices, join_grads(): lax.all_gather(first, 'row', axis=0, tiled=True)  356 us
    psum x1, waiting for transfers between devices, on_device(): lax.psum(mix_grad.astype(jnp.bfloat16), 'dp').astype(jnp.float32)  272 us
    all_to_all x1, blocking collectives, join_rows(): lax.all_to_all(jnp.stack([values] * lax.axis_size('row')), 'row', 0, 0)  166 us
    reduce_scatter x1, waiting for transfers between devices, grads_to_rows(): lax.psum_scatter(term(jnp.int32(0), lax.axis_size('row') * out_rows).asty...  128 us
  transfers between devices with their start and end apart: 15, of which 14 were waited for; matrix products, arithmetic and copies ran while one was open for 3% of the time, Pallas kernels for 0%

profile of v1, /device:TPU:0, one launch (start us, length us, event | category | flops | bytes accessed | tf_op | source)
XLA Modules:
  0.0 4360.7 jit_solution(11294304532631077148)
XLA Ops:
  8.8 13.5 psum.133
  25.4 28.5 all-gather.7.cloned.1.call-done
  56.9 22.5 fusion.207
  84.8 718.6 %reduce-scatter.10.cloned.1.call-done = f32[448,6144]{1,0:T(8,128)} async-done(((f32[1792,6144]{1,0:T(8,128)}), f32[448,6144]{1,0:T(8,128)}) %reduce-scatter.10.cloned.1.call-update) | async-done | bytes 11010064 | tf_op jit(solution)/shard_map/reduce_scatter | solution.py:135
  803.4 13.4 copy.432
  816.8 7.0 slice.128
  823.8 9.0 reshape.1405
  832.9 17.4 fusion.161
  850.3 7.0 copy.433
  874.3 405.6 %while.44 = (s32[]{:T(128)}, f32[1,8,128,256]{3,2,1,0:T(8,128)}, f32[7,1,8,64,256]{4,2,3,0,1:T(8,128)}, f32[7,1,8,128,256]{4,3,2,1,0:T(8,128)}, f32[7,1,8,64]{3,...) while((s32[]{:T(128)}, f32[1,8,128,256]{3,2,1,0:T(8,128)}, ...), condition=%wide.region_9.11_spmd.clone.clone, body=%wide.region_6.10_spmd.clone.clone.sunk | while | flops 908922432 | bytes 18620180 | solution.py:89
  877.6 40.0 custom-call.26
  933.9 40.0 custom-call.26
  992.0 40.0 custom-call.26
  1050.2 40.0 custom-call.26
  1108.3 40.0 custom-call.26
  1166.5 40.0 custom-call.26
  1224.7 40.0 custom-call.26
  1288.2 165.8 %all_to_all.5 = bf16[4,448,2048]{2,1,0:T(8,128)(2,1)S(1)} all-to-all(bf16[4,448,2048]{2,1,0:T(8,128)(2,1)S(1)} %stack.2), channel_id=1, replica_groups=mesh['dp'=4,'row'=4,'col'=2] {'row'}, dimensions={0} | all-to-all | bytes 14680064 | tf_op jit(solution)/shard_map/all_to_all | solution.py:142
  1462.6 28.0 reduce-scatter.12.cloned.1.call-done
  1492.4 11.7 psum.134
  1506.9 15.3 all-gather.11.cloned.1.call-done
  1522.2 10.0 convolution_convert_fusion
  1532.2 22.2 all-gather.9.cloned.1.call-done
  1554.4 10.2 convolution_convert_fusion.1
  1564.6 7.8 convolution_convert_fusion.2
  1572.4 1000.2 %all-reduce.31.cloned.1.call-done = (bf16[1792,2816]{1,0:T(8,128)(2,1)}, bf16[1792,2816]{1,0:T(8,128)(2,1)}, bf16[1792,2816]{1,0:T(8,128)(2,1)}) async-done(((bf16[1792,2816]{1,0:T(8,128)(2,1)}, bf16[1792,2816]{1,0:T(8,128)(2,1)}, bf16[1792,2816]{1,0:T(8,128)(2,1)}), (bf16[1792,2816]{1,0:T(8,128)(2,1)}, bf16[1792,2816]{1,0:T(8,128)(2,1)}, bf16[1792,2816]{1,0:T(8,128)(2,1)})) %all-reduce.31.cloned.1.call-update) | async-done | bytes 30277648 | tf_op jit(solution)/shard_map/psum | solution.py:247
  2572.6 18.8 fusion.155
  2591.4 8.2 fusion.208
  2599.9 8.5 add_convert_fusion.2
  2608.5 27.9 reduce-scatter.16.cloned.1.call-done
  2639.0 11.7 psum.138
  2654.0 27.1 all-gather.13.cloned.1.call-done
  2681.1 9.1 convolution_convert_fusion.4
  2690.3 127.8 %reduce-scatter.18.cloned.1.call-done = bf16[448,2048]{1,0:T(8,128)(2,1)} async-done(((bf16[1792,2048]{1,0:T(8,128)(2,1)}), bf16[448,2048]{1,0:T(8,128)(2,1)}) %reduce-scatter.18.cloned.1.call-update) | async-done | bytes 1835024 | tf_op jit(solution)/shard_map/reduce_scatter | solution.py:185
  2820.1 8.4 multiply_reduce_fusion.8
  2840.4 547.9 %while.43 = (s32[]{:T(128)}, f32[1,8,128,256]{2,3,1,0:T(8,128)}, f32[7,1,8,64,128]{4,2,3,0,1:T(8,128)}, f32[7,1,8,64,128]{4,2,3,0,1:T(8,128)}, f32[7,1,8,64,256]...) while((s32[]{:T(128)}, f32[1,8,128,256]{2,3,1,0:T(8,128)}, ...), condition=%wide.region_35.37_spmd.clone, body=%wide.region_23.36_spmd.clone.sunk | while | flops 2448786944 | bytes 53756548 | solution.py:89
  2851.0 40.7 custom-call.25
  2929.3 40.7 custom-call.25
  3007.7 40.7 custom-call.25
  3086.1 40.7 custom-call.25
  3164.4 40.7 custom-call.25
  3242.8 40.7 custom-call.25
  3321.2 40.7 custom-call.25
  3402.2 9.0 reshape.1418
  3411.2 17.4 multiply_reduce_fusion.7
  3428.6 8.2 multiply_multiply_fusion.2
  3436.8 9.3 fusion.158
  3446.1 10.1 copy.436
  3456.2 7.2 add_convert_fusion
  3471.3 13.7 all-gather
  3488.5 356.3 %all-gather.15.cloned.1.call-done = bf16[1792,6144]{1,0:T(8,128)(2,1)} async-done(((bf16[448,6144]{1,0:T(8,128)(2,1)}), bf16[1792,6144]{1,0:T(8,128)(2,1)}) %all-gather.15.cloned.1.call-update) | async-done | bytes 22020112 | tf_op jit(solution)/shard_map/all_gather | solution.py:148
  3844.9 19.4 add_convert_fusion.1
  3864.3 9.8 convolution_convert_fusion.10
  3874.2 11.6 convolution_convert_fusion.6
  3885.9 10.9 convolution_convert_fusion.5
  3896.8 7.0 convolution_convert_fusion.7
  3909.0 17.9 convolution_convert_fusion.3
  3929.1 11.2 psum.142
  3941.2 30.6 all-reduce.29.cloned.1.call-done
  3973.2 28.8 reduce-scatter.20.cloned.1.call-done
  4004.0 40.0 all-reduce.22
  4044.1 10.6 psum.139
  4060.7 271.9 %all-reduce.33.cloned.1.call-done = (bf16[512,6144]{1,0:T(8,128)(2,1)}, bf16[2048,512]{1,0:T(8,128)(2,1)}, bf16[512,2816]{1,0:T(8,128)(2,1)}, bf16[512,2816]{1,0:T(8,128)(2,1)}, bf16[2816,512]{1,0:T(8,128)(2,1)}) async-done(((bf16[512,6144]{1,0:T(8,128)(2,1)}, bf16[2048,512]{1,0:T(8,128)(2,1)}, bf16[512,2816]{1,0:T(8,128)(2,1)}, bf16[512,2816]{1,0:T(8,128)(2,1)}, bf16[2816,512]{1,0:T(8,128)(2,1)}), ...) | async-done | bytes 17039376 | tf_op jit(solution)/shard_map/psum | solution.py:279
  4332.6 9.4 convert_element_type.248
  (966 shorter events, 511.4 us)
Async XLA Ops:
  7.2 1557.4 %copy-start = (bf16[512,2816]{1,0:T(8,128)(2,1)S(1)}, bf16[512,2816]{1,0:T(8,128)(2,1)}, u32[]{:S(2)}) copy-start(bf16[512,2816]{1,0:T(8,128)(2,1)} %param.32) | copy-start | bytes 8650756
  7.2 46.6 %copy-start.51 = (bf16[512,16]{0,1:T(8,128)(2,1)S(1)}, bf16[512,16]{0,1:T(8,128)(2,1)}, u32[]{:S(2)}) copy-start(bf16[512,16]{0,1:T(8,128)(2,1)} %param.25) | copy-start | bytes 49156
  7.2 46.6 %all-gather.7.cloned.1.call-start = ((), (), s32[]{:S(2)}) async-start(), calls=%async_computation.8 | async-start | bytes 2752512 | tf_op jit(solution)/shard_map/all_gather | solution.py:126
  25.3 56.9 %reduce-scatter.22.cloned.1.call-start = ((), (), s32[]{:S(2)}) async-start(), calls=%async_computation.20 | async-start | bytes 1146880
  56.9 746.5 %reduce-scatter.10.cloned.1.call-start = ((), (), s32[]{:S(2)}) async-start(), calls=%async_computation.9 | async-start | bytes 55050240 | tf_op jit(solution)/shard_map/reduce_scatter | solution.py:135
  79.5 1411.1 %reduce-scatter.12.cloned.1.call-start = ((), (), s32[]{:S(2)}) async-start(), calls=%async_computation.10 | async-start | bytes 2752512 | tf_op jit(solution)/shard_map/reduce_scatter | solution.py:158
  80.3 736.5 %copy-start.72 = (f32[8]{0:T(128)}, f32[8]{0:T(128)S(1)}, u32[]{:S(2)}) copy-start(f32[8]{0:T(128)S(1)} %exponential_negate_fusion) | copy-start | bytes 100
  80.4 752.4 %copy-start.58 = (f32[1,448]{1,0:T(1,128)}, f32[1,448]{1,0:T(1,128)S(1)}, u32[]{:S(2)}) copy-start(f32[1,448]{1,0:T(1,128)S(1)} %get-tuple-element.925) | copy-start | bytes 5380
  80.4 752.4 %copy-start.60 = (f32[1,448]{1,0:T(1,128)}, f32[1,448]{1,0:T(1,128)S(1)}, u32[]{:S(2)}) copy-start(f32[1,448]{1,0:T(1,128)S(1)} %get-tuple-element.926) | copy-start | bytes 5380
  80.4 752.4 %copy-start.62 = (f32[1,448]{1,0:T(1,128)}, f32[1,448]{1,0:T(1,128)S(1)}, u32[]{:S(2)}) copy-start(f32[1,448]{1,0:T(1,128)S(1)} %get-tuple-element.927) | copy-start | bytes 5380
  80.5 752.3 %copy-start.32 = (f32[1,4096]{1,0:T(1,128)}, f32[1,4096]{1,0:T(1,128)S(1)}, u32[]{:S(2)}) copy-start(f32[1,4096]{1,0:T(1,128)S(1)} %get-tuple-element.917) | copy-start | bytes 49156
  80.5 752.3 %copy-start.34 = (f32[1,4096]{1,0:T(1,128)}, f32[1,4096]{1,0:T(1,128)S(1)}, u32[]{:S(2)}) copy-start(f32[1,4096]{1,0:T(1,128)S(1)} %get-tuple-element.918) | copy-start | bytes 49156
  80.5 752.3 %copy-start.36 = (f32[1,4096]{1,0:T(1,128)}, f32[1,4096]{1,0:T(1,128)S(1)}, u32[]{:S(2)}) copy-start(f32[1,4096]{1,0:T(1,128)S(1)} %get-tuple-element.919) | copy-start | bytes 49156
  80.5 752.3 %copy-start.38 = (f32[1,4096]{1,0:T(1,128)}, f32[1,4096]{1,0:T(1,128)S(1)}, u32[]{:S(2)}) copy-start(f32[1,4096]{1,0:T(1,128)S(1)} %get-tuple-element.920) | copy-start | bytes 49156
  83.3 733.5 %copy-start.40 = (f32[1,448,8,1]{1,3,2,0:T(1,128)}, f32[1,448,8,1]{1,3,2,0:T(1,128)S(1)}, u32[]{:S(2)}) copy-start(f32[1,448,8,1]{1,3,2,0:T(1,128)S(1)} %get-tuple-element.921) | copy-start | bytes 43012
  83.9 732.9 %copy-start.30 = (f32[1,7,64,8]{2,1,3,0:T(8,128)}, f32[1,7,64,8]{2,1,3,0:T(8,128)S(1)}, u32[]{:S(2)}) copy-start(f32[1,7,64,8]{2,1,3,0:T(8,128)S(1)} %squeeze.150) | copy-start | bytes 43012
  1288.1 168.7 %copy-start.76 = (bf16[2048,512]{1,0:T(8,128)(2,1)S(1)}, bf16[2048,512]{1,0:T(8,128)(2,1)}, u32[]{:S(2)}) copy-start(bf16[2048,512]{1,0:T(8,128)(2,1)} %param.30) | copy-start | bytes 6291460
  1461.9 42.2 copy-start.64
  1461.9 60.2 %all-gather.11.cloned.1.call-start = ((), (), s32[]{:S(2)}) async-start(), calls=%async_computation.13 | async-start | bytes 2752512 | tf_op jit(solution)/shard_map/all_gather | solution.py:130
  1462.5 91.8 %all-gather.9.cloned.1.call-start = ((), (), s32[]{:S(2)}) async-start(), calls=%async_computation.11 | async-start | bytes 2752512 | tf_op jit(solution)/shard_map/all_gather | solution.py:126
  1504.1 1146.6 %copy-start.49 = (f32[896]{0:T(1024)}, f32[896]{0:T(1024)S(1)}, u32[]{:S(2)}) copy-start(f32[896]{0:T(1024)S(1)} %add_rsqrt_fusion.2) | copy-start | bytes 10756
  1506.9 1065.7 %all-reduce.31.cloned.1.call-start = ((), (), s32[]{:S(2)}) async-start(), calls=%async_computation.21 | async-start | bytes 60555264 | tf_op jit(solution)/shard_map/psum | solution.py:247
  1572.4 1064.0 %reduce-scatter.16.cloned.1.call-start = ((), (), s32[]{:S(2)}) async-start(), calls=%async_computation.14 | async-start | bytes 2752512 | tf_op jit(solution)/shard_map/reduce_scatter | solution.py:172
  2599.9 36.5 copy-start.10
  2599.9 36.5 copy-start.13
  2608.4 42.3 copy-start.20
  2608.4 72.6 %all-gather.13.cloned.1.call-start = ((), (), s32[]{:S(2)}) async-start(), calls=%async_computation.15 | async-start | bytes 2752512 | tf_op jit(solution)/shard_map/all_gather | solution.py:130
  2650.7 39.5 copy-start.56
  2653.5 164.6 %reduce-scatter.18.cloned.1.call-start = ((), (), s32[]{:S(2)}) async-start(), calls=%async_computation.16 | async-start | bytes 9175040 | tf_op jit(solution)/shard_map/reduce_scatter | solution.py:185
  2690.3 1154.6 %all-gather.15.cloned.1.call-start = ((), (), s32[]{:S(2)}) async-start(), calls=%async_computation.17 | async-start | bytes 27525120 | tf_op jit(solution)/shard_map/all_gather | solution.py:148
  2846.3 48.9 %copy-start.3 = (f32[1,8,64,128]{3,2,1,0:T(8,128)}, f32[1,8,64,128]{3,2,1,0:T(8,128)S(1)}, u32[]{:S(2)}) copy-start(f32[1,8,64,128]{3,2,1,0:T(8,128)S(1)} %dynamic-slice_bitcast_fusion.18) | copy-start | bytes 786436 | tf_op jit(solution)/shard_map/transpose(jvp())/while
  2849.4 49.1 %copy-start.6 = (f32[8,64,64]{2,1,0:T(8,128)}, f32[8,64,64]{2,1,0:T(8,128)S(1)}, u32[]{:S(2)}) copy-start(f32[8,64,64]{2,1,0:T(8,128)S(1)} %fusion.368) | copy-start | bytes 393220 | tf_op jit(solution)/shard_map/transpose(jvp())/while
  2923.5 50.2 %copy-start.3 = (f32[1,8,64,128]{3,2,1,0:T(8,128)}, f32[1,8,64,128]{3,2,1,0:T(8,128)S(1)}, u32[]{:S(2)}) copy-start(f32[1,8,64,128]{3,2,1,0:T(8,128)S(1)} %dynamic-slice_bitcast_fusion.18) | copy-start | bytes 786436 | tf_op jit(solution)/shard_map/transpose(jvp())/while
  2927.8 49.1 %copy-start.6 = (f32[8,64,64]{2,1,0:T(8,128)}, f32[8,64,64]{2,1,0:T(8,128)S(1)}, u32[]{:S(2)}) copy-start(f32[8,64,64]{2,1,0:T(8,128)S(1)} %fusion.368) | copy-start | bytes 393220 | tf_op jit(solution)/shard_map/transpose(jvp())/while
  3001.8 50.2 %copy-start.3 = (f32[1,8,64,128]{3,2,1,0:T(8,128)}, f32[1,8,64,128]{3,2,1,0:T(8,128)S(1)}, u32[]{:S(2)}) copy-start(f32[1,8,64,128]{3,2,1,0:T(8,128)S(1)} %dynamic-slice_bitcast_fusion.18) | copy-start | bytes 786436 | tf_op jit(solution)/shard_map/transpose(jvp())/while
  3006.1 49.1 %copy-start.6 = (f32[8,64,64]{2,1,0:T(8,128)}, f32[8,64,64]{2,1,0:T(8,128)S(1)}, u32[]{:S(2)}) copy-start(f32[8,64,64]{2,1,0:T(8,128)S(1)} %fusion.368) | copy-start | bytes 393220 | tf_op jit(solution)/shard_map/transpose(jvp())/while
  3080.2 50.2 %copy-start.3 = (f32[1,8,64,128]{3,2,1,0:T(8,128)}, f32[1,8,64,128]{3,2,1,0:T(8,128)S(1)}, u32[]{:S(2)}) copy-start(f32[1,8,64,128]{3,2,1,0:T(8,128)S(1)} %dynamic-slice_bitcast_fusion.18) | copy-start | bytes 786436 | tf_op jit(solution)/shard_map/transpose(jvp())/while
  3084.5 49.1 %copy-start.6 = (f32[8,64,64]{2,1,0:T(8,128)}, f32[8,64,64]{2,1,0:T(8,128)S(1)}, u32[]{:S(2)}) copy-start(f32[8,64,64]{2,1,0:T(8,128)S(1)} %fusion.368) | copy-start | bytes 393220 | tf_op jit(solution)/shard_map/transpose(jvp())/while
  3158.5 50.2 %copy-start.3 = (f32[1,8,64,128]{3,2,1,0:T(8,128)}, f32[1,8,64,128]{3,2,1,0:T(8,128)S(1)}, u32[]{:S(2)}) copy-start(f32[1,8,64,128]{3,2,1,0:T(8,128)S(1)} %dynamic-slice_bitcast_fusion.18) | copy-start | bytes 786436 | tf_op jit(solution)/shard_map/transpose(jvp())/while
  3162.8 49.1 %copy-start.6 = (f32[8,64,64]{2,1,0:T(8,128)}, f32[8,64,64]{2,1,0:T(8,128)S(1)}, u32[]{:S(2)}) copy-start(f32[8,64,64]{2,1,0:T(8,128)S(1)} %fusion.368) | copy-start | bytes 393220 | tf_op jit(solution)/shard_map/transpose(jvp())/while
  3236.9 50.2 %copy-start.3 = (f32[1,8,64,128]{3,2,1,0:T(8,128)}, f32[1,8,64,128]{3,2,1,0:T(8,128)S(1)}, u32[]{:S(2)}) copy-start(f32[1,8,64,128]{3,2,1,0:T(8,128)S(1)} %dynamic-slice_bitcast_fusion.18) | copy-start | bytes 786436 | tf_op jit(solution)/shard_map/transpose(jvp())/while
  3241.2 49.1 %copy-start.6 = (f32[8,64,64]{2,1,0:T(8,128)}, f32[8,64,64]{2,1,0:T(8,128)S(1)}, u32[]{:S(2)}) copy-start(f32[8,64,64]{2,1,0:T(8,128)S(1)} %fusion.368) | copy-start | bytes 393220 | tf_op jit(solution)/shard_map/transpose(jvp())/while
  3315.3 50.2 %copy-start.3 = (f32[1,8,64,128]{3,2,1,0:T(8,128)}, f32[1,8,64,128]{3,2,1,0:T(8,128)S(1)}, u32[]{:S(2)}) copy-start(f32[1,8,64,128]{3,2,1,0:T(8,128)S(1)} %dynamic-slice_bitcast_fusion.18) | copy-start | bytes 786436 | tf_op jit(solution)/shard_map/transpose(jvp())/while
  3319.6 49.1 %copy-start.6 = (f32[8,64,64]{2,1,0:T(8,128)}, f32[8,64,64]{2,1,0:T(8,128)S(1)}, u32[]{:S(2)}) copy-start(f32[8,64,64]{2,1,0:T(8,128)S(1)} %fusion.368) | copy-start | bytes 393220 | tf_op jit(solution)/shard_map/transpose(jvp())/while
  3411.2 17.4 copy-start.35
  3411.2 17.4 copy-start.37
  3411.2 17.4 copy-start.39
  3470.2 501.5 %all-reduce.29.cloned.1.call-start = ((), (), s32[]{:S(2)}) async-start(), calls=%async_computation.19 | async-start | bytes 262144 | tf_op jit(solution)/shard_map/psum | solution.py:290
  3488.5 513.5 %reduce-scatter.20.cloned.1.call-start = ((), (), s32[]{:S(2)}) async-start(), calls=%async_computation.18 | async-start | bytes 2752512 | tf_op jit(solution)/shard_map/reduce_scatter | solution.py:172
  3864.3 192.6 %reduce-scatter.14.cloned.1.call-start = ((), (), s32[]{:S(2)}) async-start(), calls=%async_computation.12 | async-start | bytes 2752512 | tf_op jit(solution)/shard_map/reduce_scatter | solution.py:158
  3874.2 458.4 %all-reduce.33.cloned.1.call-start = ((), (), s32[]{:S(2)}) async-start(), calls=%async_computation.22 | async-start | bytes 34078720 | tf_op jit(solution)/shard_map/psum | solution.py:279
  3874.2 22.5 slice-start
  3874.2 29.6 slice-start.3
  3885.9 17.9 slice-start.4
  3926.9 75.0 %copy-start.11 = (bf16[896,512]{1,0:T(8,128)(2,1)S(1)}, bf16[896,512]{1,0:T(8,128)(2,1)}, u32[]{:S(2)}) copy-start(bf16[896,512]{1,0:T(8,128)(2,1)} %param.21) | copy-start | bytes 2752516
  3926.9 75.0 %copy-start.54 = (f32[896]{0:T(1024)S(1)}, f32[896]{0:T(1024)}, u32[]{:S(2)}) copy-start(f32[896]{0:T(1024)} %copy-done.53) | copy-start | bytes 10756
  3926.9 75.0 %copy-start.66 = (f32[512]{0:T(512)S(1)}, f32[512]{0:T(512)}, u32[]{:S(2)}) copy-start(f32[512]{0:T(512)} %param.23) | copy-start | bytes 6148
  3927.0 77.0 %copy-start.69 = (f32[512]{0:T(512)S(1)}, f32[512]{0:T(512)}, u32[]{:S(2)}) copy-start(f32[512]{0:T(512)} %get-tuple-element.811) | copy-start | bytes 6148
  3927.0 77.1 %copy-start.74 = (f32[256]{0:T(256)S(1)}, f32[256]{0:T(256)}, u32[]{:S(2)}) copy-start(f32[256]{0:T(256)} %get-tuple-element.801) | copy-start | bytes 3076
  3927.0 129.9 %copy-start.14 = (bf16[896,512]{1,0:T(8,128)(2,1)S(1)}, bf16[896,512]{1,0:T(8,128)(2,1)}, u32[]{:S(2)}) copy-start(bf16[896,512]{1,0:T(8,128)(2,1)} %reduce-scatter.12.cloned.1.call-done) | copy-start | bytes 2752516
  3927.0 129.9 %copy-start.21 = (bf16[896,512]{1,0:T(8,128)(2,1)S(1)}, bf16[896,512]{1,0:T(8,128)(2,1)}, u32[]{:S(2)}) copy-start(bf16[896,512]{1,0:T(8,128)(2,1)} %param.35) | copy-start | bytes 2752516
  3927.0 129.9 %copy-start.50 = (f32[896]{0:T(1024)S(1)}, f32[896]{0:T(1024)}, u32[]{:S(2)}) copy-start(f32[896]{0:T(1024)} %copy-done.49) | copy-start | bytes 10756
  3927.0 129.9 %copy-start.57 = (f32[896]{0:T(1024)S(1)}, f32[896]{0:T(1024)}, u32[]{:S(2)}) copy-start(f32[896]{0:T(1024)} %copy-done.56) | copy-start | bytes 10756
  3927.0 129.9 %copy-start.65 = (f32[512]{0:T(512)S(1)}, f32[512]{0:T(512)}, u32[]{:S(2)}) copy-start(f32[512]{0:T(512)} %param.31) | copy-start | bytes 6148
  (81 other events, 419.3 us)
Sparse Core Ops, SparseCore 0:
  25.4 28.3 all-gather.6
  57.0 25.0 reduce-scatter.21
  84.5 718.8 reduce-scatter.9
  1462.1 28.4 reduce-scatter.11
  1492.0 30.1 all-gather.10
  1524.2 30.1 all-gather.8
  1572.5 1000.0 all-reduce.30
  2608.6 27.7 reduce-scatter.15
  2653.6 27.3 all-gather.12
  2690.4 127.7 reduce-scatter.17
  3470.3 374.4 all-gather.14
  3850.8 120.8 all-reduce.28
  3974.0 27.9 reduce-scatter.19
  4004.2 29.4 reduce-scatter.13
  4037.7 294.8 all-reduce.32
